TPU v7x, 768 devices: a whole 4x8x12 slice. The times are simulated.
768 devices in a mesh: lat: 24 (over z_lo, y), rad: 32 (over x, z_hi, core).
Axes of the slice: x: 4, y: 8, z: 12 (z_hi: 4, z_lo: 3; z = z_hi * 3 + z_lo), core: 2. Of those that a mesh axis runs over, the one named last changes fastest.
Arguments:
- displacement: float32 [3, 128, 1536, 384], P(None, 'rad', 'lat'), may hold values from -6 to 6
- forcing: float32 [3, 128, 1536, 384], P(None, 'rad', 'lat'), may hold values from -12 to 12
- layer_id: int32 [128], P('rad'), may hold values from 0 to 11
- stiffness: float32 [12], replicated, may hold values from 0.3 to 3
- coupling: float32 [12, 3, 3], replicated, may hold values from -0.5 to 0.5
- cycle_id: int32 [1536, 384], P('lat'), may hold values from 0 to 1535, as said below
- cycle_count: int32 [1536], replicated, may hold values from 192 to 576, as said below
- gravity: float32 [2, 2, 512], replicated, may hold values from -96 to 96
Outputs:
- smoothed: float32 [3, 128, 1536, 384], P(None, 'rad', 'lat')
- potential: float32 [2, 1536, 384], P(None, 'lat')
Inputs may be any that keep to these rules, and one draw needn't show every extreme that they name: Every cycle holds at least one point, and cycle_id never falls along the lateral points taken row by row. cycle_count[j] is the number of points whose cycle_id is j.
All inputs are finite; a program needn't handle non-finite values.
Results may differ from a plain program's by a relative error of at most 0.0001.
Values sent between devices are 32-bit elements; how exact they have to be, the bound alone decides.
A program may use at most 64 MiB of HBM per device.

v0:
```python
import math

import jax
import jax.numpy as jnp
from jax import lax
from jax.sharding import PartitionSpec as P

SWEEPS = 2


OMEGA = 0.8
HIGHEST = lax.Precision.HIGHEST


def with_halo(block, sides, width):
    for axis, dim in sides:
        count = lax.axis_size(axis)
        forward = [(i, i + 1) for i in range(count - 1)]
        backward = [(target, source) for source, target in forward]
        low = lax.ppermute(
            lax.slice_in_dim(block, block.shape[dim] - width, None, axis=dim), axis, forward
        )
        high = lax.ppermute(lax.slice_in_dim(block, 0, width, axis=dim), axis, backward)
        block = jnp.concatenate([low, block, high], axis=dim)
    return block


def zonal_table(degrees, cycle_span, cycle_total):
    degree = jnp.arange(degrees, dtype=jnp.int32)[:, None]
    cycle_index = jnp.arange(cycle_span, dtype=jnp.int32)[None, :]
    phases = degree * (2 * cycle_index + 1) % (4 * cycle_total)
    return jnp.cos(jnp.pi * phases.astype(jnp.float32) / (2.0 * cycle_total))


def material(layer_id, stiffness, coupling):
    matches = layer_id[:, None] == jnp.arange(stiffness.shape[0], dtype=jnp.int32)[None, :]
    layer_mu = jnp.sum(jnp.where(matches, stiffness[None, :], 0.0), axis=1)
    layer_coupling = jnp.sum(jnp.where(matches[:, :, None, None], coupling[None], 0.0), axis=1)
    return (layer_mu, layer_coupling)


def apply_operator(padded, layer_mu, layer_coupling):
    center = padded[:, 1:-1, 1:-1, 1:-1]
    beside = padded[:, 2:, 1:-1, 1:-1] + padded[:, :-2, 1:-1, 1:-1]
    beside = beside + padded[:, 1:-1, 2:, 1:-1] + padded[:, 1:-1, :-2, 1:-1]
    beside = beside + padded[:, 1:-1, 1:-1, 2:] + padded[:, 1:-1, 1:-1, :-2]
    coupled = jnp.einsum("rcd,drab->crab", layer_coupling, center, precision=HIGHEST)
    return layer_mu[None, :, None, None] * (6.0 * center - beside) + coupled


def diagonal_of(layer_mu, layer_coupling):
    own = jnp.transpose(jnp.diagonal(layer_coupling, axis1=1, axis2=2))
    return 6.0 * layer_mu[None, :, None, None] + own[:, :, None, None]


def pad_columns(values):
    return jnp.pad(values, ((0, 0), (0, 0), (0, 0), (1, 1)))


def local(displacement, forcing, layer_id, stiffness, coupling, cycle_id, cycle_count, gravity):
    layer_mu, layer_coupling = material(layer_id, stiffness, coupling)
    diagonal = diagonal_of(layer_mu, layer_coupling)
    rad_index = lax.axis_index("rad")
    rad_count = lax.axis_size("rad")
    current = displacement
    for sweep_index in range(SWEEPS):
        padded = with_halo(current, (("lat", 2), ("rad", 1)), 1)
        padded = pad_columns(padded)
        current = (
            current
            + OMEGA * (forcing - apply_operator(padded, layer_mu, layer_coupling)) / diagonal
        )
    surface = jnp.where(rad_index == rad_count - 1, current[0, -1], 0.0)
    bottom = jnp.where(rad_index == 0, current[0, 0], 0.0)
    boundary = jnp.stack([surface, bottom])
    cycle_total = cycle_count.shape[0]
    degrees = gravity.shape[2]
    scale = math.sqrt(2.0 / cycle_total)
    flat_ids = cycle_id.reshape(-1)
    cycle_sums = jax.vmap(
        lambda row_values: jax.ops.segment_sum(row_values, flat_ids, num_segments=cycle_total)
    )(boundary.reshape(2, -1))
    basis = zonal_table(degrees, cycle_total, cycle_total)
    totals = lax.psum(cycle_sums, ("lat", "rad"))
    cycle_means = totals / cycle_count.astype(jnp.float32)[None, :]
    coefficients = scale * jnp.dot(cycle_means, basis.T, precision=HIGHEST)
    modes = gravity[:, 0] * coefficients[0][None, :] + gravity[:, 1] * coefficients[1][None, :]
    cycle_potential = scale * jnp.dot(modes, basis, precision=HIGHEST)
    potential = jnp.take(cycle_potential, cycle_id, axis=1)
    return (current, potential)


def solution(mesh):
    in_specs = (
        P(None, "rad", "lat", None),
        P(None, "rad", "lat", None),
        P("rad"),
        P(),
        P(),
        P("lat", None),
        P(),
        P(),
    )
    out_specs = (P(None, "rad", "lat", None), P(None, "lat", None))
    return jax.shard_map(local, mesh=mesh, in_specs=in_specs, out_specs=out_specs, check_vma=False)
```

profile of v0, /device:TPU:1, one launch (start us, length us, event | category | flops | bytes accessed | tf_op | source)
XLA Modules:
  0.0 512.9 jit_solution(5174649603453351669)
XLA Ops:
  0.6 0.0 copy-start
  0.6 0.0 copy-start.11
  0.7 0.0 copy-start.12
  0.7 0.0 copy-start.3
  0.7 0.0 copy-start.8
  0.7 2.2 copy.79
  2.9 0.0 copy-start.1
  2.9 1.2 copy-done.1
  4.0 4.0 collective-permute-start
  8.1 1.3 collective-permute-start.1
  9.4 0.0 copy-done.11
  9.4 0.1 iota_compare_fusion.2
  9.5 0.0 copy-done.12
  9.5 0.2 select_reduce_fusion.1
  9.7 0.0 copy-done.3
  9.7 0.0 copy-done.8
  9.7 0.1 select_reduce_fusion
  9.8 0.1 copy.87
  9.9 0.0 collective-permute-done
  10.0 0.0 copy-done
  10.0 1.0 copy_dynamic-update-slice_fusion
  10.9 1.7 collective-permute-done.1
  12.7 0.9 fusion.55
  13.6 10.8 %collective-permute-start.2 = (f32[3,1,66,384]{3,0,2,1:T(4,128)}, f32[3,1,66,384]{3,0,2,1:T(4,128)S(1)}, u32[]{:S(2)}, u32[]{:S(2)}) collective-permute-start(f32[3,1,66,384]{3,0,2,1:T(4,128)} %get-tuple-element.13), channel_id=1, source_target_pairs={{1,0},{2,1},{3,2},{4,3},{5,4},{6,5},{7,6},{8,7},{9,8},{10,9},{11,1... | collective-permute-start | bytes 912392 | tf_op jit(solution)/shard_map/ppermute | solution.py:23
  24.4 1.9 collective-permute-start.3
  26.3 0.6 gather_fusion
  26.9 0.1 copy.78
  27.0 1.9 collective-permute-done.2
  28.9 2.2 collective-permute-done.3
  31.1 0.0 copy-done.4
  31.1 0.7 copy-done.5
  31.9 2.7 select_maximum_fusion.4
  34.6 0.0 copy-done.2
  34.6 0.0 copy-done.9
  34.6 0.0 copy-start.6
  34.6 0.0 copy-start.7
  34.6 7.5 %divide_add_fusion.1 = f32[3,4,64,384]{3,0,2,1:T(4,128)S(1)} fusion(f32[3,4,64,384]{3,0,2,1:T(4,128)S(1)} %copy-done.2, f32[3,4,64,384]{3,2,1,0:T(8,128)S(1)} %copy-done.9, f32[3,6,66,386]{3,0,2,1:T(4,128)S(1)} %select_maximum_fusion.4, f32[3,4,1,384]{3,0,2,1:T(4,128)S(1)} %collective-permute-done, f32[3,4,1,384]{3,0,2,1:T(4,128)S(1)} %collective-permute-done.1, ...), kind=kOutput, calls=%fused_computation.26 | convolution fusion | flops 15630336 | bytes 10940928 | tf_op jit(solution)/shard_map/rcd,drab->crab/dot_general | solution.py:47
  42.2 1.3 collective-permute-start.5
  43.5 6.1 %collective-permute-start.4 = (f32[3,4,1,384]{3,0,2,1:T(4,128)S(1)}, f32[3,4,1,384]{3,0,2,1:T(4,128)S(1)}, u32[]{:S(2)}, u32[]{:S(2)}) collective-permute-start(f32[3,4,1,384]{3,0,2,1:T(4,128)S(1)} %get-tuple-element.16), channel_id=1, source_target_pairs={{0,32},{32,64},{64,96},{96,128},{128,160},{160,192},{192,224},{224... | collective-permute-start | bytes 55304 | tf_op jit(solution)/shard_map/ppermute | solution.py:20
  49.6 0.0 copy-done.6
  49.7 0.0 copy-done.7
  49.7 0.0 collective-permute-done.5
  49.7 0.8 collective-permute-done.4
  50.5 0.2 pad_maximum_fusion.12
  50.8 1.9 collective-permute-start.6
  52.7 5.6 %collective-permute-start.7 = (f32[3,1,66,384]{3,0,2,1:T(4,128)S(1)}, f32[3,1,66,384]{3,0,2,1:T(4,128)S(1)}, u32[]{:S(2)}, u32[]{:S(2)}) collective-permute-start(f32[3,1,66,384]{3,0,2,1:T(4,128)S(1)} %get-tuple-element.10), channel_id=1, source_target_pairs={{0,1},{1,2},{2,3},{3,4},{4,5},{5,6},{6,7},{7,8},{8,9},{9,10},{10,1... | collective-permute-start | bytes 912392 | tf_op jit(solution)/shard_map/ppermute | solution.py:20
  58.4 0.0 copy-start.10
  58.4 3.5 collective-permute-done.6
  61.9 1.1 collective-permute-done.7
  63.0 4.0 select_maximum_fusion
  67.0 0.0 copy-done.10
  67.0 9.3 %divide_add_fusion = f32[3,4,64,384]{3,0,2,1:T(4,128)S(1)} fusion(f32[3,4,64,384]{3,0,2,1:T(4,128)S(1)} %divide_add_fusion.1, f32[3,4,64,384]{3,2,1,0:T(8,128)S(1)} %copy-done.10, f32[3,6,66,386]{3,0,2,1:T(4,128)S(1)} %select_maximum_fusion, f32[3,4,1,384]{3,0,2,1:T(4,128)S(1)} %collective-permute-done.4, f32[3,4,1,384]{3,0,2,1:T(4,128)S(1)} %collective-permute-done.5, ...), kind=kOutput, calls=%fused_computation.25 | convolution fusion | flops 16809984 | bytes 9521664 | tf_op jit(solution)/shard_map/rcd,drab->crab/dot_general | solution.py:47
  76.3 1.1 copy.86
  77.5 0.2 broadcast_select_fusion.1
  77.6 0.2 maximum_bitcast_fusion
  77.8 6.9 %copy.83 = f32[24576,2]{1,0:T(8,128)} copy(f32[24576,2]{0,1:T(2,128)S(1)} %maximum_bitcast_fusion) | data formatting | bytes 393216 | tf_op jit(solution)/shard_map/stack | solution.py:75
  84.7 169.7 %scatter_custom_fusion = f32[2,1536]{0,1:T(8,128)S(1)} fusion(s32[24576]{0:T(1024)S(1)} %reshape.95, f32[24576,2]{1,0:T(8,128)} %copy.83, f32[]{:T(128)} %constant.21.clone.1), kind=kCustom, calls=%fused_computation.69 | custom fusion | flops 49152 | bytes 12800 | tf_op jit(solution)/shard_map/vmap()/scatter-add | solution.py:81
  254.5 139.4 %psum.7 = f32[2,1536]{0,1:T(8,128)S(1)} all-reduce(f32[2,1536]{0,1:T(8,128)S(1)} %scatter_custom_fusion), channel_id=1, replica_groups=mesh['lat'=24,'rad'=32] {'lat','rad'}, use_global_device_ids=true, to_apply=%region_3.4 | all-reduce | flops 3072 | bytes 24576 | tf_op jit(solution)/shard_map/psum | solution.py:84
  393.8 14.7 %fusion.36 = f32[2,512]{1,0:T(2,128)S(1)} fusion(s32[1536]{0:T(1024)S(1)} %multiply_add_fusion, f32[2,1536]{0,1:T(8,128)S(1)} %psum.7, f32[1536]{0:T(1024)S(1)} %convert_element_type.11), kind=kOutput, calls=%fused_computation.63 | convolution fusion | flops 25956352 | bytes 28672 | tf_op jit(solution)/shard_map/dot_general | solution.py:86
  408.5 13.9 %fusion.11 = f32[2,1536]{1,0:T(2,128)S(1)} fusion(s32[1536]{0:T(1024)S(1)} %multiply_add_fusion, f32[2,1,512]{2,1,0:T(1,128)S(1)} %get-tuple-element.21, f32[2,1,512]{2,1,0:T(1,128)S(1)} %get-tuple-element.20, f32[512]{0:T(512)S(1)} %bitcast.38, f32[512]{0:T(512)S(1)} %bitcast.37), kind=kOutput, calls=%fused_computation.22 | convolution fusion | flops 25958400 | bytes 30720 | tf_op jit(solution)/shard_map/dot_general | solution.py:88
  422.4 0.3 copy.84
  422.7 81.9 %gather_fusion.1 = f32[24576,2]{1,0:T(8,128)} fusion(f32[2,1536]{0,1:T(8,128)S(1)} %copy.84, s32[24576]{0:T(1024)S(1)} %broadcast_clamp_fusion), kind=kCustom, calls=%fused_computation.1 | custom fusion | bytes 491520 | tf_op jit(solution)/shard_map/jit(_take)/gather | solution.py:89
  504.6 7.6 %copy.85 = f32[64,384,2]{1,0,2:T(8,128)S(1)} copy(f32[64,384,2]{2,1,0:T(8,128)} %bitcast.33) | data formatting | bytes 393216 | tf_op jit(solution)/shard_map/jit(_take)/gather | solution.py:89
  512.2 0.7 select_bitcast_fusion
  (20 shorter events, 0.2 us)
Async XLA Ops:
  0.6 9.3 %copy-start = (f32[3,4,64,384]{3,2,1,0:T(8,128)S(1)}, f32[3,4,64,384]{3,2,1,0:T(8,128)}, u32[]{:S(2)}) copy-start(f32[3,4,64,384]{3,2,1,0:T(8,128)} %param.8) | copy-start | bytes 3538948
  0.6 8.7 %copy-start.11 = (s32[4]{0:T(128)S(1)}, s32[4]{0:T(128)}, u32[]{:S(2)}) copy-start(s32[4]{0:T(128)} %param.10) | copy-start | bytes 52
  0.7 8.8 %copy-start.12 = (f32[12]{0:T(128)S(1)}, f32[12]{0:T(128)}, u32[]{:S(2)}) copy-start(f32[12]{0:T(128)} %param.11) | copy-start | bytes 148
  0.7 9.0 %copy-start.3 = (s32[64,384]{1,0:T(8,128)S(1)}, s32[64,384]{1,0:T(8,128)}, u32[]{:S(2)}) copy-start(s32[64,384]{1,0:T(8,128)} %param.13) | copy-start | bytes 294916
  0.7 9.1 %copy-start.8 = (f32[12,3,3]{0,2,1:T(4,128)S(1)}, f32[12,3,3]{0,2,1:T(4,128)}, u32[]{:S(2)}) copy-start(f32[12,3,3]{0,2,1:T(4,128)} %param.12) | copy-start | bytes 1300
  2.9 1.2 copy-start.1
  4.0 5.9 %collective-permute-start = (f32[3,4,1,384]{3,0,2,1:T(4,128)S(1)}, f32[3,4,1,384]{3,0,2,1:T(4,128)S(1)}, u32[]{:S(2)}, u32[]{:S(2)}) collective-permute-start(f32[3,4,1,384]{3,0,2,1:T(4,128)S(1)} %get-tuple-element.19), channel_id=1, source_target_pairs={{0,32},{32,64},{64,96},{96,128},{128,160},{160,192},{192,224},{224... | collective-permute-start | bytes 55304 | tf_op jit(solution)/shard_map/ppermute | solution.py:20
  8.1 4.6 collective-permute-start.1
  13.6 15.4 %collective-permute-start.2 = (f32[3,1,66,384]{3,0,2,1:T(4,128)}, f32[3,1,66,384]{3,0,2,1:T(4,128)S(1)}, u32[]{:S(2)}, u32[]{:S(2)}) collective-permute-start(f32[3,1,66,384]{3,0,2,1:T(4,128)} %get-tuple-element.13), channel_id=1, source_target_pairs={{1,0},{2,1},{3,2},{4,3},{5,4},{6,5},{7,6},{8,7},{9,8},{10,9},{11,1... | collective-permute-start | bytes 912392 | tf_op jit(solution)/shard_map/ppermute | solution.py:23
  24.4 6.8 %collective-permute-start.3 = (f32[3,1,66,384]{3,0,2,1:T(4,128)S(1)}, f32[3,1,66,384]{3,0,2,1:T(4,128)S(1)}, u32[]{:S(2)}, u32[]{:S(2)}) collective-permute-start(f32[3,1,66,384]{3,0,2,1:T(4,128)S(1)} %get-tuple-element.12), channel_id=1, source_target_pairs={{0,1},{1,2},{2,3},{3,4},{4,5},{5,6},{6,7},{7,8},{8,9},{9,10},{10,1... | collective-permute-start | bytes 912392 | tf_op jit(solution)/shard_map/ppermute | solution.py:20
  27.0 7.6 %copy-start.2 = (f32[3,4,64,384]{3,0,2,1:T(4,128)S(1)}, f32[3,4,64,384]{3,0,2,1:T(4,128)}, u32[]{:S(2)}) copy-start(f32[3,4,64,384]{3,0,2,1:T(4,128)} %copy-done.1) | copy-start | bytes 3538948
  27.0 7.6 %copy-start.9 = (f32[3,4,64,384]{3,2,1,0:T(8,128)S(1)}, f32[3,4,64,384]{3,2,1,0:T(8,128)}, u32[]{:S(2)}) copy-start(f32[3,4,64,384]{3,2,1,0:T(8,128)} %param.9) | copy-start | bytes 3538948
  28.9 2.2 copy-start.4
  31.1 0.8 copy-start.5
  34.6 15.0 %copy-start.6 = (f32[2,2,512]{2,1,0:T(2,128)S(1)}, f32[2,2,512]{2,1,0:T(2,128)}, u32[]{:S(2)}) copy-start(f32[2,2,512]{2,1,0:T(2,128)} %param.15) | copy-start | bytes 24580
  34.6 15.1 %copy-start.7 = (s32[1536]{0:T(1024)S(1)}, s32[1536]{0:T(1024)}, u32[]{:S(2)}) copy-start(s32[1536]{0:T(1024)} %param.14) | copy-start | bytes 18436
  42.2 7.5 %collective-permute-start.5 = (f32[3,4,1,384]{3,0,2,1:T(4,128)S(1)}, f32[3,4,1,384]{3,0,2,1:T(4,128)S(1)}, u32[]{:S(2)}, u32[]{:S(2)}) collective-permute-start(f32[3,4,1,384]{3,0,2,1:T(4,128)S(1)} %get-tuple-element.17), channel_id=1, source_target_pairs={{32,0},{64,32},{96,64},{128,96},{160,128},{192,160},{224,192},{256... | collective-permute-start | bytes 55304 | tf_op jit(solution)/shard_map/ppermute | solution.py:23
  43.5 7.1 %collective-permute-start.4 = (f32[3,4,1,384]{3,0,2,1:T(4,128)S(1)}, f32[3,4,1,384]{3,0,2,1:T(4,128)S(1)}, u32[]{:S(2)}, u32[]{:S(2)}) collective-permute-start(f32[3,4,1,384]{3,0,2,1:T(4,128)S(1)} %get-tuple-element.16), channel_id=1, source_target_pairs={{0,32},{32,64},{64,96},{96,128},{128,160},{160,192},{192,224},{224... | collective-permute-start | bytes 55304 | tf_op jit(solution)/shard_map/ppermute | solution.py:20
  50.8 11.1 %collective-permute-start.6 = (f32[3,1,66,384]{3,0,2,1:T(4,128)S(1)}, f32[3,1,66,384]{3,0,2,1:T(4,128)S(1)}, u32[]{:S(2)}, u32[]{:S(2)}) collective-permute-start(f32[3,1,66,384]{3,0,2,1:T(4,128)S(1)} %get-tuple-element.11), channel_id=1, source_target_pairs={{1,0},{2,1},{3,2},{4,3},{5,4},{6,5},{7,6},{8,7},{9,8},{10,9},{11,1... | collective-permute-start | bytes 912392 | tf_op jit(solution)/shard_map/ppermute | solution.py:23
  52.7 10.3 %collective-permute-start.7 = (f32[3,1,66,384]{3,0,2,1:T(4,128)S(1)}, f32[3,1,66,384]{3,0,2,1:T(4,128)S(1)}, u32[]{:S(2)}, u32[]{:S(2)}) collective-permute-start(f32[3,1,66,384]{3,0,2,1:T(4,128)S(1)} %get-tuple-element.10), channel_id=1, source_target_pairs={{0,1},{1,2},{2,3},{3,4},{4,5},{5,6},{6,7},{7,8},{8,9},{9,10},{10,1... | collective-permute-start | bytes 912392 | tf_op jit(solution)/shard_map/ppermute | solution.py:20
  58.4 8.6 %copy-start.10 = (f32[3,4,64,384]{3,2,1,0:T(8,128)S(1)}, f32[3,4,64,384]{3,2,1,0:T(8,128)}, u32[]{:S(2)}) copy-start(f32[3,4,64,384]{3,2,1,0:T(8,128)} %param.9) | copy-start | bytes 3538948
where the time goes:
time: 518 us; the launch traced here: 513 us
  other arithmetic  178 us (34%)
  blocking collectives  139 us (27%)
  local copies, waits for them, and re-layouts  105 us (20%)
  matrix products  45.4 us (9%)
  starting transfers between devices  33 us (6%)
  waiting for transfers between devices  11.3 us (2%)
    scatter-add x1, other arithmetic, local(): jax.ops.segment_sum(row_values, flat_ids, num_segments=cycle_total)  170 us
    psum x1, blocking collectives, local(): totals = lax.psum(cycle_sums, ('lat', 'rad'))  139 us
    gather x2, local copies, waits for them, and re-layouts, local(): potential = jnp.take(cycle_potential, cycle_id, axis=1)  89.5 us
    ppermute x4, starting transfers between devices, with_halo(): lax.ppermute(lax.slice_in_dim(block, block.shape[dim] - width, None, axis...  17.7 us
    dot_general x2, matrix products, apply_operator(): jnp.einsum('rcd,drab->crab', layer_coupling, center, precision=HIGHEST)  16.9 us
    ppermute x4, starting transfers between devices, with_halo(): lax.ppermute(lax.slice_in_dim(block, 0, width, axis=dim), axis, backward)  15.3 us
    dot_general x1, matrix products, local(): coefficients = scale * jnp.dot(cycle_means, basis.T, precision=HIGHEST)  14.7 us
    dot_general x1, matrix products, local(): cycle_potential = scale * jnp.dot(modes, basis, precision=HIGHEST)  13.9 us
  transfers between devices with their start and end apart: 8, of which 6 were waited for; matrix products, arithmetic and copies ran while one was open for 0% of the time, Pallas kernels for 0%

commit v1 on v0

v1 whole, which is shorter than its diff:
```python
import functools
import math

import jax
import jax.numpy as jnp
from jax import lax
from jax.experimental import pallas as pl
from jax.experimental.pallas import tpu as pltpu
from jax.sharding import PartitionSpec as P

OMEGA = 0.8
PAD = 8
CHUNKS = 4
SLOTS = 3
MESH = pl.DeviceIdType.MESH


def sides(padded, rows):
    width = padded.shape[1]
    up = pltpu.roll(padded, 1, 0)[PAD : PAD + rows]
    down = pltpu.roll(padded, rows + 2 * PAD - 1, 0)[PAD : PAD + rows]
    center = padded[PAD : PAD + rows]
    column = lax.broadcasted_iota(jnp.int32, center.shape, 1)
    left = jnp.where(column == 0, 0.0, pltpu.roll(center, 1, 1))
    right = jnp.where(column == width - 1, 0.0, pltpu.roll(center, width - 1, 1))
    return center, (up + down) + (left + right)


def relax(factors, layer, c, centers, beside, source):
    def factor(t):
        return factors[layer - 1, 4 * c + t : 4 * c + t + 1, :]

    own = (1.0 - OMEGA) * centers[c] + factor(0) * beside + factor(1) * source
    return own + factor(2) * centers[(c + 1) % 3] + factor(3) * centers[(c + 2) % 3]


def sweep_rows(field, factors, forces, layer, row, rows):
    centers, besides = [], []
    for c in range(3):
        padded = field[c, layer, pl.ds(row, rows + 2 * PAD), :]
        center, lateral = sides(padded, rows)
        inner = pl.ds(row + PAD, rows)
        besides.append(lateral + (field[c, layer - 1, inner, :] + field[c, layer + 1, inner, :]))
        centers.append(center)
    return [
        relax(factors, layer, c, centers, besides[c], forces[c, layer - 1, pl.ds(row, rows), :])
        for c in range(3)
    ]


def sine(z):
    z2 = z * z
    poly = 1.0
    for k in (6, 5, 4, 3, 2, 1):
        poly = 1.0 - poly * z2 * (1.0 / ((2 * k) * (2 * k + 1)))
    return z * poly


def kernel(
    sizes,
    disp, force, ids_in, count_in, gravity_in, layer_in, stiffness_in, coupling_in,
    smooth_out, pot_out,
    layer_id, stiffness, coupling, u0, u1, forces, ids, counts, gravity, factors, basis, plane, force_halo,
    weights, part_y, part_z, coef,
    load_sem, lat0_send, lat0_recv, fh_send, fh_recv, rad0_send, rad0_recv,
    rad1_send, rad1_recv, lat1_send, lat1_recv, y_send, y_recv, z_send, z_recv,
    coef_send, coef_recv,
):
    n_lat, n_rad, n_y = sizes
    n_z = n_lat // n_y
    depth, height = disp.shape[1], disp.shape[2]
    total = counts.shape[0]
    degrees = gravity.shape[2]
    rows = height // CHUNKS
    top = height + PAD
    lat = lax.axis_index("lat")
    rad = lax.axis_index("rad")
    y = lat % n_y
    z = lat // n_y
    has_low, has_high = lat > 0, lat < n_lat - 1
    has_below, has_above = rad > 0, rad < n_rad - 1
    at_end = jnp.logical_or(rad == 0, rad == n_rad - 1)
    is_top = rad // (n_rad - 1)
    edge = 1 + (depth - 1) * is_top
    within = 2 + (depth - 3) * is_top
    barrier = pltpu.get_barrier_semaphore()

    def greet(where):
        pl.semaphore_signal(barrier, inc=1, device_id=where, device_id_type=MESH)

    def remote(src, dst, send, recv, where):
        return pltpu.make_async_remote_copy(
            src_ref=src, dst_ref=dst, send_sem=send, recv_sem=recv,
            device_id=where, device_id_type=MESH,
        )

    loads = [
        pltpu.make_async_copy(disp, u0.at[:, 1 : depth + 1, PAD:top, :], load_sem.at[0]),
        pltpu.make_async_copy(force, forces, load_sem.at[1]),
        pltpu.make_async_copy(ids_in, ids, load_sem.at[2]),
        pltpu.make_async_copy(count_in, counts, load_sem.at[3]),
        pltpu.make_async_copy(gravity_in, gravity, load_sem.at[4]),
        pltpu.make_async_copy(layer_in, layer_id, load_sem.at[5]),
        pltpu.make_async_copy(stiffness_in, stiffness, load_sem.at[6]),
        pltpu.make_async_copy(coupling_in, coupling, load_sem.at[7]),
    ]

    @pl.when(has_low)
    def _():
        greet((lat - 1, rad))

    @pl.when(has_high)
    def _():
        greet((lat + 1, rad))

    @pl.when(has_below)
    def _():
        greet((lat, rad - 1))
        greet((lat, 0))

    @pl.when(has_above)
    def _():
        greet((lat, rad + 1))
        greet((lat, n_rad - 1))

    @pl.when(at_end)
    def _():
        @pl.loop(1, n_y)
        def _(i):
            greet((z * n_y + (y + i) % n_y, rad))

        @pl.loop(1, n_z)
        def _(i):
            greet((((z + i) % n_z) * n_y + y, rad))

    for load in loads:
        load.start()

    for field in (u0, u1):
        @pl.when(jnp.logical_not(has_low))
        def _():
            field[:, 1 : depth + 1, 0:PAD, :] = jnp.zeros((3, depth, PAD, disp.shape[3]), jnp.float32)

        @pl.when(jnp.logical_not(has_high))
        def _():
            field[:, 1 : depth + 1, top : top + PAD, :] = jnp.zeros((3, depth, PAD, disp.shape[3]), jnp.float32)

        @pl.when(jnp.logical_not(has_below))
        def _():
            field[:, 0] = jnp.zeros((3, top + PAD, disp.shape[3]), jnp.float32)

        @pl.when(jnp.logical_not(has_above))
        def _():
            field[:, depth + 1] = jnp.zeros((3, top + PAD, disp.shape[3]), jnp.float32)

    for load in loads:
        load.wait()

    wide = (1, disp.shape[3])
    materials = lax.broadcasted_iota(jnp.int32, (3, coupling.shape[2]), 1)
    for r in range(depth):
        mu = jnp.full(wide, stiffness[layer_id[r]], jnp.float32)
        for c in range(3):
            row = jnp.sum(
                jnp.where(materials == layer_id[r], coupling[c], 0.0), axis=1, keepdims=True
            )

            def pair(d):
                return jnp.broadcast_to(row[d : d + 1], wide)

            scale = OMEGA / (6.0 * mu + pair(c))
            factors[r, 4 * c : 4 * c + 1, :] = scale * mu
            factors[r, 4 * c + 1 : 4 * c + 2, :] = scale
            factors[r, 4 * c + 2 : 4 * c + 3, :] = -scale * pair((c + 1) % 3)
            factors[r, 4 * c + 3 : 4 * c + 4, :] = -scale * pair((c + 2) % 3)

    below = (rad + n_rad - 1) // n_rad
    above = (2 * n_rad - 2 - rad) // n_rad
    lateral = (lat + n_lat - 1) // n_lat + (2 * n_lat - 2 - lat) // n_lat
    peers = (n_y - 1) + (n_z - 1) + (n_rad - 1)
    pl.semaphore_wait(barrier, lateral + below + above + (1 - below * above) * peers)

    bottom_rows, top_rows = pl.ds(PAD, PAD), pl.ds(height, PAD)
    low_halo, high_halo = pl.ds(0, PAD), pl.ds(top, PAD)

    def lat_copies(field, layers, send, recv):
        layers = pl.ds(*layers)
        up = remote(
            field.at[:, layers, top_rows, :], field.at[:, layers, low_halo, :],
            send(0), recv(0), (lat + 1, rad),
        )
        down = remote(
            field.at[:, layers, bottom_rows, :], field.at[:, layers, high_halo, :],
            send(1), recv(1), (lat - 1, rad),
        )
        return up, down

    def force_copies():
        up = remote(
            forces.at[0, edge - 1, pl.ds(height - PAD, PAD), :], force_halo.at[0],
            fh_send.at[0], fh_recv.at[0], (lat + 1, rad),
        )
        down = remote(
            forces.at[0, edge - 1, pl.ds(0, PAD), :], force_halo.at[1],
            fh_send.at[1], fh_recv.at[1], (lat - 1, rad),
        )
        return up, down

    def start_lat(copies):
        up, down = copies

        @pl.when(has_high)
        def _():
            up.start()

        @pl.when(has_low)
        def _():
            down.start()

    def arrive_lat(copies):
        up, down = copies

        @pl.when(has_low)
        def _():
            up.wait_recv()

        @pl.when(has_high)
        def _():
            down.wait_recv()

    def leave_lat(copies):
        up, down = copies

        @pl.when(has_high)
        def _():
            up.wait_send()

        @pl.when(has_low)
        def _():
            down.wait_send()

    def chunk_of(i):
        return (CHUNKS - i) % CHUNKS

    def rad_up(field, send, recv, i):
        at = pl.ds(pl.multiple_of(PAD + chunk_of(i) * rows, 8), rows)
        return remote(
            field.at[:, depth, at, :], field.at[:, 0, at, :],
            send.at[0, i], recv.at[0, i], (lat, rad + 1),
        )

    def rad_down(field, send, recv, i):
        at = pl.ds(pl.multiple_of(PAD + chunk_of(i) * rows, 8), rows)
        return remote(
            field.at[:, 1, at, :], field.at[:, depth + 1, at, :],
            send.at[1, i], recv.at[1, i], (lat, rad - 1),
        )

    lat0 = lat_copies(u0, (1, depth), lambda d: lat0_send.at[d], lambda d: lat0_recv.at[d])
    start_lat(lat0)

    @pl.when(at_end)
    def _():
        start_lat(force_copies())

    for i in range(CHUNKS):
        @pl.when(has_above)
        def _():
            rad_up(u0, rad0_send, rad0_recv, i).start()

        @pl.when(has_below)
        def _():
            rad_down(u0, rad0_send, rad0_recv, i).start()

    first = ids[:, 0:1]
    degree = lax.broadcasted_iota(jnp.int32, (height, degrees), 1).astype(jnp.float32)
    period = 4.0 * total
    for k in range(SLOTS):
        odd = (2 * (first + k) + 1).astype(jnp.float32)
        phase = degree * odd
        phase = phase - period * jnp.floor(phase * (1.0 / period) + 0.5)
        basis[k] = sine((total - jnp.abs(phase)) * (math.pi / (2.0 * total)))

    @pl.when(at_end)
    def _():
        cycle = lax.broadcasted_iota(jnp.int32, (height, total), 1)
        for k in range(SLOTS):
            found = jnp.where(cycle == first + k, counts[...].reshape(1, total), 0)
            count = jnp.sum(found.astype(jnp.float32), axis=1, keepdims=True)
            weights[k] = jnp.where(count > 0.0, 1.0 / jnp.maximum(count, 1.0), 0.0)

    arrive_lat(lat0)

    @pl.loop(0, (depth - 2) * CHUNKS)
    def _(i):
        layer = 2 + i // CHUNKS
        row = pl.multiple_of((i % CHUNKS) * rows, 8)
        values = sweep_rows(u0, factors, forces, layer, row, rows)
        for c in range(3):
            u1[c, layer, pl.ds(row + PAD, rows), :] = values[c]

    lat1 = [
        lat_copies(
            u1, layers, lambda d, part=part: lat1_send.at[d, part],
            lambda d, part=part: lat1_recv.at[d, part],
        )
        for part, layers in enumerate(((2, depth - 2), (1, 1), (depth, 1)))
    ]
    start_lat(lat1[0])

    def y_copy(i):
        return remote(
            part_y.at[y], part_y.at[y], y_send.at[i], y_recv.at[y],
            (z * n_y + (y + i) % n_y, rad),
        )

    def y_arrival(i):
        other = (y + i) % n_y
        return remote(
            part_y.at[other], part_y.at[other], y_send.at[i], y_recv.at[other],
            (z * n_y + other, rad),
        )

    def z_copy(i):
        return remote(
            part_z.at[z], part_z.at[z], z_send.at[i], z_recv.at[z],
            (((z + i) % n_z) * n_y + y, rad),
        )

    def z_arrival(i):
        other = (z + i) % n_z
        return remote(
            part_z.at[other], part_z.at[other], z_send.at[i], z_recv.at[other],
            (other * n_y + y, rad),
        )

    def coef_copy(i):
        return remote(
            coef.at[is_top], coef.at[is_top], coef_send.at[i], coef_recv.at[is_top],
            (lat, (rad + i) % n_rad),
        )

    @pl.when(at_end)
    def _():
        arrive_lat(force_copies())

        @pl.loop(0, CHUNKS)
        def _(i):
            row = pl.multiple_of(i * rows, 8)
            values = sweep_rows(u0, factors, forces, edge, row, rows)
            for c in range(3):
                u1[c, edge, pl.ds(row + PAD, rows), :] = values[c]
            plane[pl.ds(row + PAD, rows), :] = values[0]

        for start, halo, inside in ((0, 0, has_low), (top, 1, has_high)):
            base = 0 if halo == 0 else top - PAD
            both = u0[0, edge, pl.ds(base, 2 * PAD), :]
            up = pltpu.roll(both, 1, 0)[start - base : start - base + PAD]
            down = pltpu.roll(both, 2 * PAD - 1, 0)[start - base : start - base + PAD]
            centers = [u0[c, edge, pl.ds(start, PAD), :] for c in range(3)]
            column = lax.broadcasted_iota(jnp.int32, centers[0].shape, 1)
            width = column.shape[1]
            left = jnp.where(column == 0, 0.0, pltpu.roll(centers[0], 1, 1))
            right = jnp.where(column == width - 1, 0.0, pltpu.roll(centers[0], width - 1, 1))
            beside = (up + down) + (left + right) + u0[0, within, pl.ds(start, PAD), :]
            value = relax(factors, edge, 0, centers, beside, force_halo[halo])
            plane[pl.ds(start, PAD), :] = jnp.where(inside, value, 0.0)

        center, lateral = sides(plane[...], height)
        own = pl.ds(PAD, height)
        centers = [center, u1[1, edge, own, :], u1[2, edge, own, :]]
        beside = lateral + u1[0, within, own, :]
        boundary = relax(factors, edge, 0, centers, beside, forces[0, edge - 1])
        partial = jnp.zeros((1, degrees), jnp.float32)
        for k in range(SLOTS):
            mine = jnp.where(ids[...] == first + k, boundary, 0.0)
            means = jnp.sum(mine, axis=1, keepdims=True) * weights[k]
            partial = partial + jnp.sum(means * basis[k], axis=0, keepdims=True)
        part_y[y] = partial

        @pl.loop(1, n_y)
        def _(i):
            y_copy(i).start()

    @pl.loop(0, CHUNKS)
    def _(i):
        row = pl.multiple_of(chunk_of(i) * rows, 8)

        @pl.when(has_above)
        def _():
            rad_down(u0, rad0_send, rad0_recv, i).wait_recv()

        values = sweep_rows(u0, factors, forces, depth, row, rows)
        for c in range(3):
            u1[c, depth, pl.ds(row + PAD, rows), :] = values[c]

        @pl.when(has_above)
        def _():
            rad_up(u1, rad1_send, rad1_recv, i).start()

        @pl.when(has_below)
        def _():
            rad_up(u0, rad0_send, rad0_recv, i).wait_recv()

        values = sweep_rows(u0, factors, forces, 1, row, rows)
        for c in range(3):
            u1[c, 1, pl.ds(row + PAD, rows), :] = values[c]

        @pl.when(has_below)
        def _():
            rad_down(u1, rad1_send, rad1_recv, i).start()

        @pl.when(i == 1)
        def _():
            start_lat(lat1[1])
            start_lat(lat1[2])

    @pl.when(at_end)
    def _():
        @pl.loop(1, n_y)
        def _(i):
            y_arrival(i).wait_recv()

        part_z[z] = jnp.sum(part_y[...], axis=0)

        @pl.loop(1, n_z)
        def _(i):
            z_copy(i).start()

    arrive_lat(lat1[0])

    @pl.loop(0, (depth - 2) * CHUNKS)
    def _(i):
        layer = 2 + i // CHUNKS
        row = pl.multiple_of((i % CHUNKS) * rows, 8)
        values = sweep_rows(u1, factors, forces, layer, row, rows)
        for c in range(3):
            smooth_out[c, layer - 1, pl.ds(row, rows), :] = values[c]

    scale = math.sqrt(2.0 / total)

    @pl.when(at_end)
    def _():
        @pl.loop(1, n_z)
        def _(i):
            z_arrival(i).wait_recv()

        coef[is_top] = scale * jnp.sum(part_z[...], axis=0)

        @pl.loop(1, n_rad)
        def _(i):
            coef_copy(i).start()

    arrive_lat(lat1[1])
    arrive_lat(lat1[2])

    @pl.loop(0, CHUNKS)
    def _(i):
        row = pl.multiple_of(chunk_of(i) * rows, 8)

        @pl.when(has_above)
        def _():
            rad_down(u1, rad1_send, rad1_recv, i).wait_recv()

        values = sweep_rows(u1, factors, forces, depth, row, rows)
        for c in range(3):
            smooth_out[c, depth - 1, pl.ds(row, rows), :] = values[c]

        @pl.when(has_below)
        def _():
            rad_up(u1, rad1_send, rad1_recv, i).wait_recv()

        values = sweep_rows(u1, factors, forces, 1, row, rows)
        for c in range(3):
            smooth_out[c, 0, pl.ds(row, rows), :] = values[c]

    def coef_arrival(side):
        return remote(
            coef.at[side], coef.at[side], coef_send.at[0], coef_recv.at[side],
            (lat, (rad + 1) % n_rad),
        )

    @pl.when(has_above)
    def _():
        coef_arrival(1).wait_recv()

    @pl.when(has_below)
    def _():
        coef_arrival(0).wait_recv()

    for k in range(2):
        modes = gravity[k, 0:1, :] * coef[1] + gravity[k, 1:2, :] * coef[0]
        values = [
            scale * jnp.sum(basis[s] * modes, axis=1, keepdims=True) for s in range(SLOTS)
        ]
        picked = jnp.where(ids[...] == first + 1, values[1], values[2])
        pot_out[k] = jnp.where(ids[...] == first, values[0], picked)

    leave_lat(lat0)
    for copies in lat1:
        leave_lat(copies)

    @pl.loop(0, CHUNKS)
    def _(i):
        @pl.when(has_above)
        def _():
            rad_up(u0, rad0_send, rad0_recv, i).wait_send()
            rad_up(u1, rad1_send, rad1_recv, i).wait_send()

        @pl.when(has_below)
        def _():
            rad_down(u0, rad0_send, rad0_recv, i).wait_send()
            rad_down(u1, rad1_send, rad1_recv, i).wait_send()

    @pl.when(at_end)
    def _():
        leave_lat(force_copies())

        @pl.loop(1, n_y)
        def _(i):
            y_copy(i).wait_send()

        @pl.loop(1, n_z)
        def _(i):
            z_copy(i).wait_send()

        @pl.loop(1, n_rad)
        def _(i):
            coef_copy(i).wait_send()


def solution(mesh):
    n_lat, n_rad = mesh.shape["lat"], mesh.shape["rad"]
    n_y = 8 if n_lat % 8 == 0 else max(1, n_lat // 2)
    n_z = n_lat // n_y

    def local(displacement, forcing, layer_id, stiffness, coupling, cycle_id, cycle_count, gravity):
        _, depth, height, width = displacement.shape
        total = cycle_count.shape[0]
        degrees = gravity.shape[2]
        vmem = pltpu.VMEM
        dma = pltpu.SemaphoreType.DMA
        f32 = jnp.float32
        field = vmem((3, depth + 2, height + 2 * PAD, width), f32)
        anywhere = pl.BlockSpec(memory_space=pl.ANY)
        inside = pl.BlockSpec(memory_space=pltpu.VMEM)
        return pl.pallas_call(
            functools.partial(kernel, (n_lat, n_rad, n_y)),
            out_shape=(
                jax.ShapeDtypeStruct(displacement.shape, f32),
                jax.ShapeDtypeStruct((2, height, width), f32),
            ),
            in_specs=[anywhere] * 8,
            out_specs=(inside, inside),
            scratch_shapes=[
                pltpu.SMEM(layer_id.shape, jnp.int32),
                pltpu.SMEM(stiffness.shape, f32),
                vmem((3, 3, stiffness.shape[0]), f32),
                field,
                field,
                vmem((3, depth, height, width), f32),
                vmem((height, width), jnp.int32),
                vmem((total,), jnp.int32),
                vmem((2, 2, degrees), f32),
                vmem((depth, 16, width), f32),
                vmem((SLOTS, height, degrees), f32),
                vmem((height + 2 * PAD, width), f32),
                vmem((2, PAD, width), f32),
                vmem((SLOTS, height, 1), f32),
                vmem((n_y, 1, degrees), f32),
                vmem((n_z, 1, degrees), f32),
                vmem((2, 1, degrees), f32),
                dma((8,)),
                dma((2,)), dma((2,)), dma((2,)), dma((2,)),
                dma((2, CHUNKS)), dma((2, CHUNKS)), dma((2, CHUNKS)), dma((2, CHUNKS)),
                dma((2, 3)), dma((2, 3)),
                dma((n_y,)), dma((n_y,)), dma((n_z,)), dma((n_z,)),
                dma((n_rad,)), dma((2,)),
            ],
            compiler_params=pltpu.CompilerParams(
                collective_id=0, has_side_effects=True, vmem_limit_bytes=40 << 20
            ),
        )(*(
            pltpu.with_memory_space_constraint(array, pltpu.HBM)
            for array in (
                displacement, forcing, cycle_id, cycle_count, gravity,
                layer_id, stiffness, jnp.transpose(coupling, (1, 2, 0)),
            )
        ))

    in_specs = (
        P(None, "rad", "lat", None),
        P(None, "rad", "lat", None),
        P("rad"),
        P(),
        P(),
        P("lat", None),
        P(),
        P(),
    )
    out_specs = (P(None, "rad", "lat", None), P(None, "lat", None))
    return jax.shard_map(local, mesh=mesh, in_specs=in_specs, out_specs=out_specs, check_vma=False)
```

time: 518 us -> 46 us (0.09)
  other arithmetic: 178 us -> 0 us
  blocking collectives: 139 us -> 0 us
  local copies, waits for them, and re-layouts: 105 us -> 1.69 us
  matrix products: 45.4 us -> 0 us
  Pallas kernels: 0 us -> 43.5 us
  starting transfers between devices: 33 us -> 0 us
  waiting for transfers between devices: 11.3 us -> 0 us
    scatter-add x1 -> x0, other arithmetic: 170 us -> none  [local(): jax.ops.segment_sum(row_values, flat_ids, num_segments=cycle_total)]
    psum x1 -> x0, blocking collectives: 139 us -> none  [local(): totals = lax.psum(cycle_sums, ('lat', 'rad'))]
    gather x3 -> x0, local copies, waits for them, and re-layouts: 90.1 us -> none  [the longest x2 89.5 us: local(): potential = jnp.take(cycle_potential, cycle_id, axis=1)]
    dot_general x4 -> x0, matrix products: 45.4 us -> none  [the longest x2 16.9 us: apply_operator(): jnp.einsum('rcd,drab->crab', layer_coupling, center, precision=HIGHEST)]
    pallas_call x0 -> x1, Pallas kernels: none -> 43.5 us  [local(): pl.pallas_call(functools.partial(kernel, (n_lat, n_rad, n_y)), out_shape=...]
    ppermute x8 -> x0, starting transfers between devices: 33 us -> none  [the longest x4 17.7 us: with_halo(): lax.ppermute(lax.slice_in_dim(block, block.shape[dim] - width, None, axis...]
    ppermute x8 -> x0, waiting for transfers between devices: 11.3 us -> none  [the longest x4 7.16 us: with_halo(): lax.ppermute(lax.slice_in_dim(block, 0, width, axis=dim), axis, backward)]
    concatenate x4 -> x0, other arithmetic: 6.9 us -> none  [the longest x3 6.89 us: with_halo(): block = jnp.concatenate([low, block, high], axis=dim)]
  transfers between devices with their start and end apart: 8 -> 0, of which waited for: 6 -> 0; matrix products, arithmetic and copies ran while one was open for 0% -> 0% of each run, Pallas kernels for 0% -> 0%
where the time goes in v1:
time: 46 us; the launch traced here: 45.8 us
  Pallas kernels  43.5 us (95%)
  local copies, waits for them, and re-layouts  1.69 us (4%)
  between operations  0.64 us (1%)
    pallas_call x1, Pallas kernels, local(): pl.pallas_call(functools.partial(kernel, (n_lat, n_rad, n_y)), out_shape=...  43.5 us
    unnamed x2, local copies, waits for them, and re-layouts  1.69 us

profile of v1, /device:TPU:1, one launch (start us, length us, event | category | flops | bytes accessed | tf_op | source)
XLA Modules:
  0.0 45.8 jit_solution(17125250997316431898)
XLA Ops:
  0.6 43.5 %shard_map.95 = (f32[3,4,64,384]{3,2,1,0:T(8,128)S(1)}, f32[2,64,384]{2,1,0:T(8,128)S(1)}) custom-call(f32[3,4,64,384]{3,2,1,0:T(8,128)} %disp.1, f32[3,4,64,384]{3,2,1,0:T(8,128)} %force.1, s32[64,384]{1,0:T(8,128)} %ids_in.1, s32[1536]{0:T(1024)} %count_in.1, f32[2,2,512]{2,1,0:T(2,128)} %gravity_in.1, s32[4]{0:T(128)} %layer_in.1, f32[12]{0:T(128)} %stiffness_in.1, ...), custom_call_target="tpu_custom_call" | custom-call | tf_op jit(solution)/shard_map/pallas_call | solution.py:547
  44.1 1.0 %copy.12 = f32[3,4,64,384]{3,2,1,0:T(8,128)} copy(f32[3,4,64,384]{3,2,1,0:T(8,128)S(1)} %get-tuple-element.4) | data formatting | bytes 2359296
  45.1 0.7 %copy.13 = f32[2,64,384]{2,1,0:T(8,128)} copy(f32[2,64,384]{2,1,0:T(8,128)S(1)} %get-tuple-element.5) | data formatting | bytes 393216

commit v2 on v1

--- a/solution.py
+++ b/solution.py
@@ -34,17 +34,21 @@
     return own + factor(2) * centers[(c + 1) % 3] + factor(3) * centers[(c + 2) % 3]
 
 
-def sweep_rows(field, factors, forces, layer, row, rows):
+def sweep_rows(field, factors, forces, layer, row, rows, components=(0, 1, 2)):
+    inner = pl.ds(row + PAD, rows)
     centers, besides = [], []
     for c in range(3):
+        if c not in components:
+            centers.append(field[c, layer, inner, :])
+            besides.append(None)
+            continue
         padded = field[c, layer, pl.ds(row, rows + 2 * PAD), :]
         center, lateral = sides(padded, rows)
-        inner = pl.ds(row + PAD, rows)
         besides.append(lateral + (field[c, layer - 1, inner, :] + field[c, layer + 1, inner, :]))
         centers.append(center)
     return [
         relax(factors, layer, c, centers, besides[c], forces[c, layer - 1, pl.ds(row, rows), :])
-        for c in range(3)
+        for c in components
     ]
 
 
@@ -60,9 +64,9 @@
     sizes,
     disp, force, ids_in, count_in, gravity_in, layer_in, stiffness_in, coupling_in,
     smooth_out, pot_out,
-    layer_id, stiffness, coupling, u0, u1, forces, ids, counts, gravity, factors, basis, plane, force_halo,
-    weights, part_y, part_z, coef,
-    load_sem, lat0_send, lat0_recv, fh_send, fh_recv, rad0_send, rad0_recv,
+    layer_id, stiffness, coupling, u0, u1, forces, ids, counts, gravity, factors, basis, plane, pack0, halo0,
+    pack1, halo1, weights, part_y, part_z, coef,
+    load_sem, lat0_send, lat0_recv, rad0_send, rad0_recv,
     rad1_send, rad1_recv, lat1_send, lat1_recv, y_send, y_recv, z_send, z_recv,
     coef_send, coef_recv,
 ):
@@ -178,66 +182,62 @@
     above = (2 * n_rad - 2 - rad) // n_rad
     lateral = (lat + n_lat - 1) // n_lat + (2 * n_lat - 2 - lat) // n_lat
     peers = (n_y - 1) + (n_z - 1) + (n_rad - 1)
-    pl.semaphore_wait(barrier, lateral + below + above + (1 - below * above) * peers)
-
-    bottom_rows, top_rows = pl.ds(PAD, PAD), pl.ds(height, PAD)
-    low_halo, high_halo = pl.ds(0, PAD), pl.ds(top, PAD)
-
-    def lat_copies(field, layers, send, recv):
-        layers = pl.ds(*layers)
-        up = remote(
-            field.at[:, layers, top_rows, :], field.at[:, layers, low_halo, :],
-            send(0), recv(0), (lat + 1, rad),
-        )
-        down = remote(
-            field.at[:, layers, bottom_rows, :], field.at[:, layers, high_halo, :],
-            send(1), recv(1), (lat - 1, rad),
-        )
-        return up, down
-
-    def force_copies():
-        up = remote(
-            forces.at[0, edge - 1, pl.ds(height - PAD, PAD), :], force_halo.at[0],
-            fh_send.at[0], fh_recv.at[0], (lat + 1, rad),
-        )
-        down = remote(
-            forces.at[0, edge - 1, pl.ds(0, PAD), :], force_halo.at[1],
-            fh_send.at[1], fh_recv.at[1], (lat - 1, rad),
-        )
-        return up, down
-
-    def start_lat(copies):
-        up, down = copies
+
+    def lat_up(pack, halo, send, recv):
+        return remote(pack.at[0], halo.at[0], send.at[0], recv.at[0], (lat + 1, rad))
+
+    def lat_down(pack, halo, send, recv):
+        return remote(pack.at[1], halo.at[1], send.at[1], recv.at[1], (lat - 1, rad))
+
+    lat0 = (pack0, halo0, lat0_send, lat0_recv)
+    lat1 = [
+        (pack1.at[part], halo1.at[part], lat1_send.at[part], lat1_recv.at[part])
+        for part in range(2)
+    ]
+    all_layers = tuple(range(1, depth + 1))
+    inner_layers, outer_layers = all_layers[1:-1], (1, depth)
+
+    def planes(layers):
+        return [(c, layer) for c in range(3) for layer in layers]
+
+    def put_rows(field, pack, side, layers):
+        row = PAD if side else top - 1
+        for place, (c, layer) in enumerate(planes(layers)):
+            pack[side, place : place + 1, :] = field[c, layer, row : row + 1, :]
+
+    def take_rows(field, copies, layers):
+        halo = copies[1]
+
+        @pl.when(has_low)
+        def _():
+            lat_up(*copies).wait_recv()
+            for place, (c, layer) in enumerate(planes(layers)):
+                field[c, layer, PAD - 1 : PAD, :] = halo[0, place : place + 1, :]
 
         @pl.when(has_high)
         def _():
-            up.start()
-
+            lat_down(*copies).wait_recv()
+            for place, (c, layer) in enumerate(planes(layers)):
+                field[c, layer, top : top + 1, :] = halo[1, place : place + 1, :]
+
+    def send_up(copies):
+        @pl.when(has_high)
+        def _():
+            lat_up(*copies).start()
+
+    def send_down(copies):
         @pl.when(has_low)
         def _():
-            down.start()
-
-    def arrive_lat(copies):
-        up, down = copies
+            lat_down(*copies).start()
+
+    def leave_lat(copies):
+        @pl.when(has_high)
+        def _():
+            lat_up(*copies).wait_send()
 
         @pl.when(has_low)
         def _():
-            up.wait_recv()
-
-        @pl.when(has_high)
-        def _():
-            down.wait_recv()
-
-    def leave_lat(copies):
-        up, down = copies
-
-        @pl.when(has_high)
-        def _():
-            up.wait_send()
-
-        @pl.when(has_low)
-        def _():
-            down.wait_send()
+            lat_down(*copies).wait_send()
 
     def chunk_of(i):
         return (CHUNKS - i) % CHUNKS
@@ -256,12 +256,30 @@
             send.at[1, i], recv.at[1, i], (lat, rad - 1),
         )
 
-    lat0 = lat_copies(u0, (1, depth), lambda d: lat0_send.at[d], lambda d: lat0_recv.at[d])
-    start_lat(lat0)
+    spare = 3 * depth
+    for side in range(2):
+        put_rows(u0, pack0, side, all_layers)
 
     @pl.when(at_end)
     def _():
-        start_lat(force_copies())
+        for side, start in ((0, top - PAD), (1, PAD)):
+            tile = pl.ds(start, PAD)
+            centers = [u0[c, edge, tile, :] for c in range(3)]
+            column = lax.broadcasted_iota(jnp.int32, centers[0].shape, 1)
+            width = column.shape[1]
+            left = jnp.where(column == 0, 0.0, pltpu.roll(centers[0], 1, 1))
+            right = jnp.where(column == width - 1, 0.0, pltpu.roll(centers[0], width - 1, 1))
+            along = pltpu.roll(centers[0], PAD - 1 if side else 1, 0)
+            beside = along + (left + right) + u0[0, within, tile, :]
+            value = relax(
+                factors, edge, 0, centers, beside, forces[0, edge - 1, pl.ds(start - PAD, PAD), :]
+            )
+            pick = 0 if side else PAD - 1
+            pack0[side, spare : spare + 1, :] = value[pick : pick + 1]
+
+    pl.semaphore_wait(barrier, lateral + below + above + (1 - below * above) * peers)
+    send_up(lat0)
+    send_down(lat0)
 
     for i in range(CHUNKS):
         @pl.when(has_above)
@@ -289,24 +307,7 @@
             count = jnp.sum(found.astype(jnp.float32), axis=1, keepdims=True)
             weights[k] = jnp.where(count > 0.0, 1.0 / jnp.maximum(count, 1.0), 0.0)
 
-    arrive_lat(lat0)
-
-    @pl.loop(0, (depth - 2) * CHUNKS)
-    def _(i):
-        layer = 2 + i // CHUNKS
-        row = pl.multiple_of((i % CHUNKS) * rows, 8)
-        values = sweep_rows(u0, factors, forces, layer, row, rows)
-        for c in range(3):
-            u1[c, layer, pl.ds(row + PAD, rows), :] = values[c]
-
-    lat1 = [
-        lat_copies(
-            u1, layers, lambda d, part=part: lat1_send.at[d, part],
-            lambda d, part=part: lat1_recv.at[d, part],
-        )
-        for part, layers in enumerate(((2, depth - 2), (1, 1), (depth, 1)))
-    ]
-    start_lat(lat1[0])
+    take_rows(u0, lat0, all_layers)
 
     def y_copy(i):
         return remote(
@@ -342,8 +343,6 @@
 
     @pl.when(at_end)
     def _():
-        arrive_lat(force_copies())
-
         @pl.loop(0, CHUNKS)
         def _(i):
             row = pl.multiple_of(i * rows, 8)
@@ -351,20 +350,13 @@
             for c in range(3):
                 u1[c, edge, pl.ds(row + PAD, rows), :] = values[c]
             plane[pl.ds(row + PAD, rows), :] = values[0]
-
-        for start, halo, inside in ((0, 0, has_low), (top, 1, has_high)):
-            base = 0 if halo == 0 else top - PAD
-            both = u0[0, edge, pl.ds(base, 2 * PAD), :]
-            up = pltpu.roll(both, 1, 0)[start - base : start - base + PAD]
-            down = pltpu.roll(both, 2 * PAD - 1, 0)[start - base : start - base + PAD]
-            centers = [u0[c, edge, pl.ds(start, PAD), :] for c in range(3)]
-            column = lax.broadcasted_iota(jnp.int32, centers[0].shape, 1)
-            width = column.shape[1]
-            left = jnp.where(column == 0, 0.0, pltpu.roll(centers[0], 1, 1))
-            right = jnp.where(column == width - 1, 0.0, pltpu.roll(centers[0], width - 1, 1))
-            beside = (up + down) + (left + right) + u0[0, within, pl.ds(start, PAD), :]
-            value = relax(factors, edge, 0, centers, beside, force_halo[halo])
-            plane[pl.ds(start, PAD), :] = jnp.where(inside, value, 0.0)
+            values = sweep_rows(u0, factors, forces, within, row, rows, (0,))
+            u1[0, within, pl.ds(row + PAD, rows), :] = values[0]
+
+        for side, inside, row, own in ((0, has_low, PAD - 1, PAD), (1, has_high, top, top - 1)):
+            value = halo0[side, spare : spare + 1, :]
+            value = value + factors[edge - 1, 0:1, :] * u0[0, edge, own : own + 1, :]
+            plane[row : row + 1, :] = jnp.where(inside, value, 0.0)
 
         center, lateral = sides(plane[...], height)
         own = pl.ds(PAD, height)
@@ -382,6 +374,19 @@
         def _(i):
             y_copy(i).start()
 
+    @pl.loop(0, (depth - 2) * CHUNKS)
+    def _(i):
+        layer = 2 + i // CHUNKS
+        row = pl.multiple_of((i % CHUNKS) * rows, 8)
+        values = sweep_rows(u0, factors, forces, layer, row, rows)
+        for c in range(3):
+            u1[c, layer, pl.ds(row + PAD, rows), :] = values[c]
+
+    for side in range(2):
+        put_rows(u1, pack1.at[0], side, inner_layers)
+    send_up(lat1[0])
+    send_down(lat1[0])
+
     @pl.loop(0, CHUNKS)
     def _(i):
         row = pl.multiple_of(chunk_of(i) * rows, 8)
@@ -410,10 +415,15 @@
         def _():
             rad_down(u1, rad1_send, rad1_recv, i).start()
 
+        @pl.when(i == 0)
+        def _():
+            put_rows(u1, pack1.at[1], 1, outer_layers)
+            send_down(lat1[1])
+
         @pl.when(i == 1)
         def _():
-            start_lat(lat1[1])
-            start_lat(lat1[2])
+            put_rows(u1, pack1.at[1], 0, outer_layers)
+            send_up(lat1[1])
 
     @pl.when(at_end)
     def _():
@@ -427,7 +437,7 @@
         def _(i):
             z_copy(i).start()
 
-    arrive_lat(lat1[0])
+    take_rows(u1, lat1[0], inner_layers)
 
     @pl.loop(0, (depth - 2) * CHUNKS)
     def _(i):
@@ -451,8 +461,7 @@
         def _(i):
             coef_copy(i).start()
 
-    arrive_lat(lat1[1])
-    arrive_lat(lat1[2])
+    take_rows(u1, lat1[1], outer_layers)
 
     @pl.loop(0, CHUNKS)
     def _(i):
@@ -514,8 +523,6 @@
 
     @pl.when(at_end)
     def _():
-        leave_lat(force_copies())
-
         @pl.loop(1, n_y)
         def _(i):
             y_copy(i).wait_send()
@@ -565,15 +572,18 @@
                 vmem((depth, 16, width), f32),
                 vmem((SLOTS, height, degrees), f32),
                 vmem((height + 2 * PAD, width), f32),
-                vmem((2, PAD, width), f32),
+                vmem((2, 16, width), f32),
+                vmem((2, 16, width), f32),
+                vmem((2, 2, 8, width), f32),
+                vmem((2, 2, 8, width), f32),
                 vmem((SLOTS, height, 1), f32),
                 vmem((n_y, 1, degrees), f32),
                 vmem((n_z, 1, degrees), f32),
                 vmem((2, 1, degrees), f32),
                 dma((8,)),
-                dma((2,)), dma((2,)), dma((2,)), dma((2,)),
+                dma((2,)), dma((2,)),
                 dma((2, CHUNKS)), dma((2, CHUNKS)), dma((2, CHUNKS)), dma((2, CHUNKS)),
-                dma((2, 3)), dma((2, 3)),
+                dma((2, 2)), dma((2, 2)),
                 dma((n_y,)), dma((n_y,)), dma((n_z,)), dma((n_z,)),
                 dma((n_rad,)), dma((2,)),
             ],

time: 46 us -> 40.9 us (0.89)
  the two profiles are of different devices: /device:TPU:1 before, /device:TPU:56 now
where the time goes in v2:
time: 40.9 us; the launch traced here: 40.7 us
  Pallas kernels  38.4 us (94%)
  local copies, waits for them, and re-layouts  1.69 us (4%)
  between operations  0.64 us (2%)
    pallas_call x1, Pallas kernels, local(): pl.pallas_call(functools.partial(kernel, (n_lat, n_rad, n_y)), out_shape=...  38.4 us
    unnamed x2, local copies, waits for them, and re-layouts  1.69 us

profile of v2, /device:TPU:56, one launch (start us, length us, event | category | flops | bytes accessed | tf_op | source)
XLA Modules:
  0.0 40.7 jit_solution(6940012153016012396)
XLA Ops:
  0.6 38.4 %shard_map.95 = (f32[3,4,64,384]{3,2,1,0:T(8,128)S(1)}, f32[2,64,384]{2,1,0:T(8,128)S(1)}) custom-call(f32[3,4,64,384]{3,2,1,0:T(8,128)} %disp.1, f32[3,4,64,384]{3,2,1,0:T(8,128)} %force.1, s32[64,384]{1,0:T(8,128)} %ids_in.1, s32[1536]{0:T(1024)} %count_in.1, f32[2,2,512]{2,1,0:T(2,128)} %gravity_in.1, s32[4]{0:T(128)} %layer_in.1, f32[12]{0:T(128)} %stiffness_in.1, ...), custom_call_target="tpu_custom_call" | custom-call | tf_op jit(solution)/shard_map/pallas_call | solution.py:554
  39.0 1.0 %copy.12 = f32[3,4,64,384]{3,2,1,0:T(8,128)} copy(f32[3,4,64,384]{3,2,1,0:T(8,128)S(1)} %get-tuple-element.4) | data formatting | bytes 2359296
  40.0 0.7 %copy.13 = f32[2,64,384]{2,1,0:T(8,128)} copy(f32[2,64,384]{2,1,0:T(8,128)S(1)} %get-tuple-element.5) | data formatting | bytes 393216

commit v3 on v2

--- a/solution.py
+++ b/solution.py
@@ -65,13 +65,12 @@
     disp, force, ids_in, count_in, gravity_in, layer_in, stiffness_in, coupling_in,
     smooth_out, pot_out,
     layer_id, stiffness, coupling, u0, u1, forces, ids, counts, gravity, factors, basis, plane, pack0, halo0,
-    pack1, halo1, weights, part_y, part_z, coef,
+    pack1, halo1, weights, part, coef,
     load_sem, lat0_send, lat0_recv, rad0_send, rad0_recv,
-    rad1_send, rad1_recv, lat1_send, lat1_recv, y_send, y_recv, z_send, z_recv,
+    rad1_send, rad1_recv, lat1_send, lat1_recv, part_send, part_recv,
     coef_send, coef_recv,
 ):
-    n_lat, n_rad, n_y = sizes
-    n_z = n_lat // n_y
+    n_lat, n_rad = sizes
     depth, height = disp.shape[1], disp.shape[2]
     total = counts.shape[0]
     degrees = gravity.shape[2]
@@ -79,8 +78,6 @@
     top = height + PAD
     lat = lax.axis_index("lat")
     rad = lax.axis_index("rad")
-    y = lat % n_y
-    z = lat // n_y
     has_low, has_high = lat > 0, lat < n_lat - 1
     has_below, has_above = rad > 0, rad < n_rad - 1
     at_end = jnp.logical_or(rad == 0, rad == n_rad - 1)
@@ -129,15 +126,11 @@
 
     @pl.when(at_end)
     def _():
-        @pl.loop(1, n_y)
+        @pl.loop(1, n_lat)
         def _(i):
-            greet((z * n_y + (y + i) % n_y, rad))
-
-        @pl.loop(1, n_z)
-        def _(i):
-            greet((((z + i) % n_z) * n_y + y, rad))
-
-    for load in loads:
+            greet(((lat + i) % n_lat, rad))
+
+    for load in loads[5:] + loads[:5]:
         load.start()
 
     for field in (u0, u1):
@@ -157,7 +150,7 @@
         def _():
             field[:, depth + 1] = jnp.zeros((3, top + PAD, disp.shape[3]), jnp.float32)
 
-    for load in loads:
+    for load in loads[5:]:
         load.wait()
 
     wide = (1, disp.shape[3])
@@ -181,7 +174,7 @@
     below = (rad + n_rad - 1) // n_rad
     above = (2 * n_rad - 2 - rad) // n_rad
     lateral = (lat + n_lat - 1) // n_lat + (2 * n_lat - 2 - lat) // n_lat
-    peers = (n_y - 1) + (n_z - 1) + (n_rad - 1)
+    peers = (n_lat - 1) + (n_rad - 1)
 
     def lat_up(pack, halo, send, recv):
         return remote(pack.at[0], halo.at[0], send.at[0], recv.at[0], (lat + 1, rad))
@@ -240,21 +233,52 @@
             lat_down(*copies).wait_send()
 
     def chunk_of(i):
-        return (CHUNKS - i) % CHUNKS
-
-    def rad_up(field, send, recv, i):
+        return i + 1 - 2 * (i % 2)
+
+    def rad_up(i):
         at = pl.ds(pl.multiple_of(PAD + chunk_of(i) * rows, 8), rows)
         return remote(
-            field.at[:, depth, at, :], field.at[:, 0, at, :],
-            send.at[0, i], recv.at[0, i], (lat, rad + 1),
-        )
-
-    def rad_down(field, send, recv, i):
+            u1.at[:, depth, at, :], u1.at[:, 0, at, :],
+            rad1_send.at[0, i], rad1_recv.at[0, i], (lat, rad + 1),
+        )
+
+    def rad_up_first(i):
+        start = chunk_of(i) * rows
+        return remote(
+            disp.at[:, depth - 1, pl.ds(start, rows), :],
+            u0.at[:, 0, pl.ds(pl.multiple_of(PAD + start, 8), rows), :],
+            rad0_send.at[0, i], rad0_recv.at[0, i], (lat, rad + 1),
+        )
+
+    def rad_down_first(i):
+        start = chunk_of(i) * rows
+        return remote(
+            disp.at[:, 0, pl.ds(start, rows), :],
+            u0.at[:, depth + 1, pl.ds(pl.multiple_of(PAD + start, 8), rows), :],
+            rad0_send.at[1, i], rad0_recv.at[1, i], (lat, rad - 1),
+        )
+
+    def rad_down(i):
         at = pl.ds(pl.multiple_of(PAD + chunk_of(i) * rows, 8), rows)
         return remote(
-            field.at[:, 1, at, :], field.at[:, depth + 1, at, :],
-            send.at[1, i], recv.at[1, i], (lat, rad - 1),
-        )
+            u1.at[:, 1, at, :], u1.at[:, depth + 1, at, :],
+            rad1_send.at[1, i], rad1_recv.at[1, i], (lat, rad - 1),
+        )
+
+    pl.semaphore_wait(barrier, lateral + below + above + (1 - below * above) * peers)
+    def send_first(chunks):
+        for i in chunks:
+            @pl.when(has_above)
+            def _():
+                rad_up_first(i).start()
+
+            @pl.when(has_below)
+            def _():
+                rad_down_first(i).start()
+
+    send_first(range(1))
+    for load in loads[:5]:
+        load.wait()
 
     spare = 3 * depth
     for side in range(2):
@@ -277,18 +301,9 @@
             pick = 0 if side else PAD - 1
             pack0[side, spare : spare + 1, :] = value[pick : pick + 1]
 
-    pl.semaphore_wait(barrier, lateral + below + above + (1 - below * above) * peers)
     send_up(lat0)
     send_down(lat0)
-
-    for i in range(CHUNKS):
-        @pl.when(has_above)
-        def _():
-            rad_up(u0, rad0_send, rad0_recv, i).start()
-
-        @pl.when(has_below)
-        def _():
-            rad_down(u0, rad0_send, rad0_recv, i).start()
+    send_first(range(1, CHUNKS))
 
     first = ids[:, 0:1]
     degree = lax.broadcasted_iota(jnp.int32, (height, degrees), 1).astype(jnp.float32)
@@ -307,32 +322,16 @@
             count = jnp.sum(found.astype(jnp.float32), axis=1, keepdims=True)
             weights[k] = jnp.where(count > 0.0, 1.0 / jnp.maximum(count, 1.0), 0.0)
 
-    take_rows(u0, lat0, all_layers)
-
-    def y_copy(i):
-        return remote(
-            part_y.at[y], part_y.at[y], y_send.at[i], y_recv.at[y],
-            (z * n_y + (y + i) % n_y, rad),
-        )
-
-    def y_arrival(i):
-        other = (y + i) % n_y
-        return remote(
-            part_y.at[other], part_y.at[other], y_send.at[i], y_recv.at[other],
-            (z * n_y + other, rad),
-        )
-
-    def z_copy(i):
-        return remote(
-            part_z.at[z], part_z.at[z], z_send.at[i], z_recv.at[z],
-            (((z + i) % n_z) * n_y + y, rad),
-        )
-
-    def z_arrival(i):
-        other = (z + i) % n_z
-        return remote(
-            part_z.at[other], part_z.at[other], z_send.at[i], z_recv.at[other],
-            (other * n_y + y, rad),
+    def part_copy(i):
+        return remote(
+            part.at[lat], part.at[lat], part_send.at[i], part_recv.at[lat],
+            ((lat + i) % n_lat, rad),
+        )
+
+    def part_arrival(i):
+        other = (lat + i) % n_lat
+        return remote(
+            part.at[other], part.at[other], part_send.at[i], part_recv.at[other], (other, rad)
         )
 
     def coef_copy(i):
@@ -343,6 +342,8 @@
 
     @pl.when(at_end)
     def _():
+        take_rows(u0, lat0, all_layers)
+
         @pl.loop(0, CHUNKS)
         def _(i):
             row = pl.multiple_of(i * rows, 8)
@@ -368,11 +369,44 @@
             mine = jnp.where(ids[...] == first + k, boundary, 0.0)
             means = jnp.sum(mine, axis=1, keepdims=True) * weights[k]
             partial = partial + jnp.sum(means * basis[k], axis=0, keepdims=True)
-        part_y[y] = partial
-
-        @pl.loop(1, n_y)
+        part[lat] = partial
+
+        @pl.loop(1, n_lat)
         def _(i):
-            y_copy(i).start()
+            part_copy(i).start()
+
+    def outer_chunk(i):
+        row = pl.multiple_of(chunk_of(i) * rows, 8)
+
+        @pl.when(has_above)
+        def _():
+            rad_down_first(i).wait_recv()
+
+        values = sweep_rows(u0, factors, forces, depth, row, rows)
+        for c in range(3):
+            u1[c, depth, pl.ds(row + PAD, rows), :] = values[c]
+
+        @pl.when(has_above)
+        def _():
+            rad_up(i).start()
+
+        @pl.when(has_below)
+        def _():
+            rad_up_first(i).wait_recv()
+
+        values = sweep_rows(u0, factors, forces, 1, row, rows)
+        for c in range(3):
+            u1[c, 1, pl.ds(row + PAD, rows), :] = values[c]
+
+        @pl.when(has_below)
+        def _():
+            rad_down(i).start()
+
+    outer_chunk(0)
+
+    @pl.when(jnp.logical_not(at_end))
+    def _():
+        take_rows(u0, lat0, all_layers)
 
     @pl.loop(0, (depth - 2) * CHUNKS)
     def _(i):
@@ -387,55 +421,27 @@
     send_up(lat1[0])
     send_down(lat1[0])
 
-    @pl.loop(0, CHUNKS)
-    def _(i):
-        row = pl.multiple_of(chunk_of(i) * rows, 8)
-
-        @pl.when(has_above)
-        def _():
-            rad_down(u0, rad0_send, rad0_recv, i).wait_recv()
-
-        values = sweep_rows(u0, factors, forces, depth, row, rows)
-        for c in range(3):
-            u1[c, depth, pl.ds(row + PAD, rows), :] = values[c]
-
-        @pl.when(has_above)
-        def _():
-            rad_up(u1, rad1_send, rad1_recv, i).start()
-
-        @pl.when(has_below)
-        def _():
-            rad_up(u0, rad0_send, rad0_recv, i).wait_recv()
-
-        values = sweep_rows(u0, factors, forces, 1, row, rows)
-        for c in range(3):
-            u1[c, 1, pl.ds(row + PAD, rows), :] = values[c]
-
-        @pl.when(has_below)
-        def _():
-            rad_down(u1, rad1_send, rad1_recv, i).start()
-
-        @pl.when(i == 0)
-        def _():
-            put_rows(u1, pack1.at[1], 1, outer_layers)
-            send_down(lat1[1])
-
-        @pl.when(i == 1)
-        def _():
-            put_rows(u1, pack1.at[1], 0, outer_layers)
-            send_up(lat1[1])
+    pl.loop(1, CHUNKS - 1)(outer_chunk)
+    for side in range(2):
+        put_rows(u1, pack1.at[1], side, outer_layers)
+    send_up(lat1[1])
+    send_down(lat1[1])
+
+    outer_chunk(CHUNKS - 1)
+
+    scale = math.sqrt(2.0 / total)
 
     @pl.when(at_end)
     def _():
-        @pl.loop(1, n_y)
+        @pl.loop(1, n_lat)
         def _(i):
-            y_arrival(i).wait_recv()
-
-        part_z[z] = jnp.sum(part_y[...], axis=0)
-
-        @pl.loop(1, n_z)
+            part_arrival(i).wait_recv()
+
+        coef[is_top] = scale * jnp.sum(part[...], axis=0)
+
+        @pl.loop(1, n_rad)
         def _(i):
-            z_copy(i).start()
+            coef_copy(i).start()
 
     take_rows(u1, lat1[0], inner_layers)
 
@@ -447,29 +453,12 @@
         for c in range(3):
             smooth_out[c, layer - 1, pl.ds(row, rows), :] = values[c]
 
-    scale = math.sqrt(2.0 / total)
-
-    @pl.when(at_end)
-    def _():
-        @pl.loop(1, n_z)
-        def _(i):
-            z_arrival(i).wait_recv()
-
-        coef[is_top] = scale * jnp.sum(part_z[...], axis=0)
-
-        @pl.loop(1, n_rad)
-        def _(i):
-            coef_copy(i).start()
-
-    take_rows(u1, lat1[1], outer_layers)
-
-    @pl.loop(0, CHUNKS)
-    def _(i):
+    def last_chunk(i):
         row = pl.multiple_of(chunk_of(i) * rows, 8)
 
         @pl.when(has_above)
         def _():
-            rad_down(u1, rad1_send, rad1_recv, i).wait_recv()
+            rad_down(i).wait_recv()
 
         values = sweep_rows(u1, factors, forces, depth, row, rows)
         for c in range(3):
@@ -477,11 +466,15 @@
 
         @pl.when(has_below)
         def _():
-            rad_up(u1, rad1_send, rad1_recv, i).wait_recv()
+            rad_up(i).wait_recv()
 
         values = sweep_rows(u1, factors, forces, 1, row, rows)
         for c in range(3):
             smooth_out[c, 0, pl.ds(row, rows), :] = values[c]
+
+    last_chunk(0)
+    take_rows(u1, lat1[1], outer_layers)
+    pl.loop(1, CHUNKS)(last_chunk)
 
     def coef_arrival(side):
         return remote(
@@ -513,33 +506,38 @@
     def _(i):
         @pl.when(has_above)
         def _():
-            rad_up(u0, rad0_send, rad0_recv, i).wait_send()
-            rad_up(u1, rad1_send, rad1_recv, i).wait_send()
+            rad_up_first(i).wait_send()
+            rad_up(i).wait_send()
 
         @pl.when(has_below)
         def _():
-            rad_down(u0, rad0_send, rad0_recv, i).wait_send()
-            rad_down(u1, rad1_send, rad1_recv, i).wait_send()
+            rad_down_first(i).wait_send()
+            rad_down(i).wait_send()
 
     @pl.when(at_end)
     def _():
-        @pl.loop(1, n_y)
+        @pl.loop(1, n_lat)
         def _(i):
-            y_copy(i).wait_send()
-
-        @pl.loop(1, n_z)
-        def _(i):
-            z_copy(i).wait_send()
+            part_copy(i).wait_send()
 
         @pl.loop(1, n_rad)
         def _(i):
             coef_copy(i).wait_send()
 
 
+def deliver(smooth, pot, smooth_out, pot_out, sems):
+    copies = [
+        pltpu.make_async_copy(smooth, smooth_out, sems.at[0]),
+        pltpu.make_async_copy(pot, pot_out, sems.at[1]),
+    ]
+    for copy in copies:
+        copy.start()
+    for copy in copies:
+        copy.wait()
+
+
 def solution(mesh):
     n_lat, n_rad = mesh.shape["lat"], mesh.shape["rad"]
-    n_y = 8 if n_lat % 8 == 0 else max(1, n_lat // 2)
-    n_z = n_lat // n_y
 
     def local(displacement, forcing, layer_id, stiffness, coupling, cycle_id, cycle_count, gravity):
         _, depth, height, width = displacement.shape
@@ -551,8 +549,8 @@
         field = vmem((3, depth + 2, height + 2 * PAD, width), f32)
         anywhere = pl.BlockSpec(memory_space=pl.ANY)
         inside = pl.BlockSpec(memory_space=pltpu.VMEM)
-        return pl.pallas_call(
-            functools.partial(kernel, (n_lat, n_rad, n_y)),
+        results = pl.pallas_call(
+            functools.partial(kernel, (n_lat, n_rad)),
             out_shape=(
                 jax.ShapeDtypeStruct(displacement.shape, f32),
                 jax.ShapeDtypeStruct((2, height, width), f32),
@@ -577,14 +575,13 @@
                 vmem((2, 2, 8, width), f32),
                 vmem((2, 2, 8, width), f32),
                 vmem((SLOTS, height, 1), f32),
-                vmem((n_y, 1, degrees), f32),
-                vmem((n_z, 1, degrees), f32),
+                vmem((n_lat, 1, degrees), f32),
                 vmem((2, 1, degrees), f32),
                 dma((8,)),
                 dma((2,)), dma((2,)),
                 dma((2, CHUNKS)), dma((2, CHUNKS)), dma((2, CHUNKS)), dma((2, CHUNKS)),
                 dma((2, 2)), dma((2, 2)),
-                dma((n_y,)), dma((n_y,)), dma((n_z,)), dma((n_z,)),
+                dma((n_lat,)), dma((n_lat,)),
                 dma((n_rad,)), dma((2,)),
             ],
             compiler_params=pltpu.CompilerParams(
@@ -597,6 +594,14 @@
                 layer_id, stiffness, jnp.transpose(coupling, (1, 2, 0)),
             )
         ))
+        return tuple(pl.pallas_call(
+            deliver,
+            out_shape=tuple(jax.ShapeDtypeStruct(array.shape, f32) for array in results),
+            in_specs=[inside, inside],
+            out_specs=(anywhere, anywhere),
+            scratch_shapes=[dma((2,))],
+            compiler_params=pltpu.CompilerParams(vmem_limit_bytes=1 << 20),
+        )(*results))
 
     in_specs = (
         P(None, "rad", "lat", None),

time: 40.9 us -> 39.6 us (0.968)
  the two profiles are of different devices: /device:TPU:56 before, /device:TPU:1 now
where the time goes in v3:
time: 39.6 us; the launch traced here: 39.1 us
  Pallas kernels  38.5 us (97%)
  between operations  0.64 us (2%)
    pallas_call x1, Pallas kernels, local(): pl.pallas_call(functools.partial(kernel, (n_lat, n_rad)), out_shape=(jax....  37.4 us
    pallas_call x1, Pallas kernels, local(): pl.pallas_call(deliver, out_shape=tuple((jax.ShapeDtypeStruct(array.shape...  1.08 us

profile of v3, /device:TPU:1, one launch (start us, length us, event | category | flops | bytes accessed | tf_op | source)
XLA Modules:
  0.0 39.1 jit_solution(5129208161997383330)
XLA Ops:
  0.6 37.4 %shard_map.95 = (f32[3,4,64,384]{3,2,1,0:T(8,128)S(1)}, f32[2,64,384]{2,1,0:T(8,128)S(1)}) custom-call(f32[3,4,64,384]{3,2,1,0:T(8,128)} %disp.1, f32[3,4,64,384]{3,2,1,0:T(8,128)} %force.1, s32[64,384]{1,0:T(8,128)} %ids_in.1, s32[1536]{0:T(1024)} %count_in.1, f32[2,2,512]{2,1,0:T(2,128)} %gravity_in.1, s32[4]{0:T(128)} %layer_in.1, f32[12]{0:T(128)} %stiffness_in.1, ...), custom_call_target="tpu_custom_call" | custom-call | tf_op jit(solution)/shard_map/pallas_call | solution.py:552
  38.0 1.1 %shard_map.96 = (f32[3,4,64,384]{3,2,1,0:T(8,128)}, f32[2,64,384]{2,1,0:T(8,128)}) custom-call(f32[3,4,64,384]{3,2,1,0:T(8,128)S(1)} %get-tuple-element.4.smooth, f32[2,64,384]{2,1,0:T(8,128)S(1)} %get-tuple-element.5.pot), custom_call_target="tpu_custom_call" | custom-call | tf_op jit(solution)/shard_map/pallas_call | solution.py:597

commit v4 on v3

--- a/solution.py
+++ b/solution.py
@@ -50,6 +50,18 @@
         relax(factors, layer, c, centers, besides[c], forces[c, layer - 1, pl.ds(row, rows), :])
         for c in components
     ]
+
+
+def ring(offset, size):
+    return min(offset, size - offset)
+
+
+def rad_hops(offset):
+    return ring(offset // 8, 4) + 3 * ring(offset // 2 % 4, 4)
+
+
+def lat_hops(offset):
+    return ring(offset % 8, 8) + ring(offset // 8, 3)
 
 
 def sine(z):
@@ -337,7 +349,7 @@
     def coef_copy(i):
         return remote(
             coef.at[is_top], coef.at[is_top], coef_send.at[i], coef_recv.at[is_top],
-            (lat, (rad + i) % n_rad),
+            (lat, i + is_top * (n_rad - 1 - 2 * i)),
         )
 
     @pl.when(at_end)
@@ -371,8 +383,7 @@
             partial = partial + jnp.sum(means * basis[k], axis=0, keepdims=True)
         part[lat] = partial
 
-        @pl.loop(1, n_lat)
-        def _(i):
+        for i in sorted(range(1, n_lat), key=lat_hops, reverse=True):
             part_copy(i).start()
 
     def outer_chunk(i):
@@ -439,8 +450,7 @@
 
         coef[is_top] = scale * jnp.sum(part[...], axis=0)
 
-        @pl.loop(1, n_rad)
-        def _(i):
+        for i in sorted(range(1, n_rad), key=rad_hops, reverse=True):
             coef_copy(i).start()
 
     take_rows(u1, lat1[0], inner_layers)

time: 39.6 us -> 39.9 us (level)
  Pallas kernels: 38.5 us -> 39.1 us
    pallas_call x1, Pallas kernels: 37.4 us -> 38 us  [local(): pl.pallas_call(functools.partial(kernel, (n_lat, n_rad)), out_shape=(jax....]
where the time goes in v4:
time: 39.9 us; the launch traced here: 39.7 us
  Pallas kernels  39.1 us (98%)
  between operations  0.64 us (2%)
    pallas_call x1, Pallas kernels, local(): pl.pallas_call(functools.partial(kernel, (n_lat, n_rad)), out_shape=(jax....  38 us
    pallas_call x1, Pallas kernels, local(): pl.pallas_call(deliver, out_shape=tuple((jax.ShapeDtypeStruct(array.shape...  1.08 us

profile of v4, /device:TPU:1, one launch (start us, length us, event | category | flops | bytes accessed | tf_op | source)
XLA Modules:
  0.0 39.7 jit_solution(13757426747543440090)
XLA Ops:
  0.6 38.0 %shard_map.95 = (f32[3,4,64,384]{3,2,1,0:T(8,128)S(1)}, f32[2,64,384]{2,1,0:T(8,128)S(1)}) custom-call(f32[3,4,64,384]{3,2,1,0:T(8,128)} %disp.1, f32[3,4,64,384]{3,2,1,0:T(8,128)} %force.1, s32[64,384]{1,0:T(8,128)} %ids_in.1, s32[1536]{0:T(1024)} %count_in.1, f32[2,2,512]{2,1,0:T(2,128)} %gravity_in.1, s32[4]{0:T(128)} %layer_in.1, f32[12]{0:T(128)} %stiffness_in.1, ...), custom_call_target="tpu_custom_call" | custom-call | tf_op jit(solution)/shard_map/pallas_call | solution.py:562
  38.6 1.1 %shard_map.96 = (f32[3,4,64,384]{3,2,1,0:T(8,128)}, f32[2,64,384]{2,1,0:T(8,128)}) custom-call(f32[3,4,64,384]{3,2,1,0:T(8,128)S(1)} %get-tuple-element.4.smooth, f32[2,64,384]{2,1,0:T(8,128)S(1)} %get-tuple-element.5.pot), custom_call_target="tpu_custom_call" | custom-call | tf_op jit(solution)/shard_map/pallas_call | solution.py:607
